TPU v7x, 256 devices: a whole 4x4x8 slice. The times are simulated.
256 devices in a mesh: mem: 32 (over x, y, core), row: 8 (over z).
Axes of the slice: x: 4, y: 4, z: 8, core: 2. Of those that a mesh axis runs over, the one named last changes fastest.
Arguments:
- predicted_surpass_tally: int32 [32, 1024, 4096], P('mem', 'row'), may hold values from 0 to 1, as said below
- observed_surpass_tally: int32 [1024, 4096], P('row'), may hold values from 0 to 1, as said below
Outputs:
- energy_maps: float32 [1, 8, 1024, 4096], P(None, None, 'row', 'mem')
- skill: float32 [32, 1, 8], P('mem')
Inputs may be any that keep to these rules, and one draw needn't show every extreme that they name: `predicted_surpass_tally`: A cell that exceeds a threshold exceeds every lower one, so the mask of threshold t is the class being greater than t. `observed_surpass_tally`: coded as predicted_surpass_tally.
All inputs are finite; a program needn't handle non-finite values.
Results may differ from a plain program's by a relative error of at most 0.0003.
Values sent between devices are 32-bit elements; how exact they have to be, the bound alone decides.
A program may use at most 64 MiB of HBM per device.

v0:
```python
import jax
import jax.numpy as jnp
from jax import lax
from jax.sharding import PartitionSpec as P

NT = 1
LEVELS = 7


KERNEL = (1.0 / 16.0, 4.0 / 16.0, 6.0 / 16.0, 4.0 / 16.0, 1.0 / 16.0)


def extended(x, sides, width):
    for axis, dim in sides:
        count, length = (lax.axis_size(axis), x.shape[dim])
        up = [(i, (i + 1) % count) for i in range(count - 1)]
        down = [(j, i) for i, j in up]
        last = lax.slice_in_dim(x, length - width, length, axis=dim)
        first = lax.slice_in_dim(x, 0, width, axis=dim)
        before = lax.ppermute(last, axis, up)
        after = lax.ppermute(first, axis, down)
        x = jnp.concatenate([before, x, after], axis=dim)
    return x


def column_pass(field, spacing):
    breadth = field.shape[1]
    padded = jnp.pad(field, ((0, 0), (2 * spacing, 2 * spacing)))
    result = KERNEL[0] * padded[:, 0:breadth]
    for index in range(1, 5):
        result = result + KERNEL[index] * padded[:, index * spacing : index * spacing + breadth]
    return result


def row_pass(padded, spacing, height):
    result = KERNEL[0] * padded[0:height]
    for index in range(1, 5):
        result = result + KERNEL[index] * padded[index * spacing : index * spacing + height]
    return result


def smooth_field(field, spacing):
    across = column_pass(field, spacing)
    padded = extended(across, (("row", 0),), 2 * spacing)
    return row_pass(padded, spacing, field.shape[0])


def decompose(field):
    pieces = []
    current = field
    for level in range(1, LEVELS + 1):
        smoother = smooth_field(current, 2 ** (level - 1))
        pieces.append(current - smoother)
        current = smoother
    pieces.append(current)
    return pieces


def on_device(predicted_surpass_tally, observed_surpass_tally):
    height, breadth = observed_surpass_tally.shape
    member_count = lax.axis_size("mem")
    cells = float(height * lax.axis_size("row") * breadth)
    realization_surpass_tally = predicted_surpass_tally[0]
    weights = [4.0 ** min(level + 1, LEVELS) for level in range(LEVELS + 1)]
    weighted = []
    cumulative_accumulations = []
    observed = (observed_surpass_tally > 0).astype(jnp.float32)
    counts = [jnp.sum(observed)]
    error_field = (realization_surpass_tally > 0).astype(jnp.float32) - observed
    pieces = decompose(error_field)
    for level in range(LEVELS + 1):
        squared = pieces[level] * pieces[level]
        weighted.append(squared * weights[level])
        cumulative_accumulations.append(jnp.sum(squared))
    local_totals = jnp.stack(cumulative_accumulations).reshape(NT, LEVELS + 1)
    local_counts = jnp.stack(counts)
    sum_totals, sum_counts = lax.psum((local_totals, local_counts), "row")
    base_rate = sum_counts / cells
    mean_error = sum_totals / cells
    spread = 2.0 * base_rate * (1.0 - base_rate)
    skill = (1.0 - mean_error * (LEVELS + 1) / spread[:, None])[None, :, :]
    stacked = jnp.stack(weighted).reshape(NT, LEVELS + 1, height, breadth)
    summed = lax.psum_scatter(stacked, "mem", scatter_dimension=3, tiled=True)
    energy_maps = summed / member_count
    return (energy_maps, skill)


def solution(mesh):
    placed = (P("mem", "row", None), P("row", None))
    return jax.shard_map(
        on_device,
        mesh=mesh,
        in_specs=placed,
        out_specs=(P(None, None, "row", "mem"), P("mem", None, None)),
        check_vma=False,
    )
```

profile of v0, /device:TPU:6, one launch (start us, length us, event | category | flops | bytes accessed | tf_op | source)
XLA Modules:
  0.0 307.7 jit_solution(5322726240747592754)
XLA Ops:
  7.2 0.0 copy-start
  7.2 0.0 reduce-scatter.2.cloned.1.call-start
  7.2 2.9 convert_reduce_fusion
  10.1 0.0 copy-done
  10.1 0.3 convert_subtract_fusion
  10.4 2.2 multiply_add_fusion.6
  12.7 3.8 %collective-permute-start = (f32[2,4096]{1,0:T(2,128)S(1)}, f32[2,4096]{1,0:T(2,128)S(1)}, u32[]{:S(2)}, u32[]{:S(2)}) collective-permute-start(f32[2,4096]{1,0:T(2,128)S(1)} %get-tuple-element.37), channel_id=1, source_target_pairs={{0,1},{1,2},{2,3},{3,4},{4,5},{5,6},{6,7},{8,9},{9,10},{10,11},{11... | collective-permute-start | bytes 98312 | tf_op jit(solution)/shard_map/ppermute | solution.py:20
  16.5 1.3 collective-permute-start.1
  17.8 0.3 collective-permute-done
  18.1 4.2 %collective-permute-done.1 = f32[2,4096]{1,0:T(2,128)S(1)} collective-permute-done((f32[2,4096]{1,0:T(2,128)S(1)}, f32[2,4096]{1,0:T(2,128)S(1)}, u32[]{:S(2)}, u32[]{:S(2)}) %collective-permute-start.1) | collective-permute-done | bytes 32800 | tf_op jit(solution)/shard_map/ppermute | solution.py:21
  22.3 2.6 bitcast_dynamic-update-slice_fusion.7
  25.0 2.2 multiply_add_fusion.5
  27.2 3.8 %collective-permute-start.2 = (f32[4,4096]{1,0:T(4,128)S(1)}, f32[4,4096]{1,0:T(4,128)S(1)}, u32[]{:S(2)}, u32[]{:S(2)}) collective-permute-start(f32[4,4096]{1,0:T(4,128)S(1)} %get-tuple-element.35), channel_id=1, source_target_pairs={{0,1},{1,2},{2,3},{3,4},{4,5},{5,6},{6,7},{8,9},{9,10},{10,11},{11... | collective-permute-start | bytes 196616 | tf_op jit(solution)/shard_map/ppermute | solution.py:20
  31.0 1.3 collective-permute-start.3
  32.3 0.6 collective-permute-done.2
  32.9 5.3 %collective-permute-done.3 = f32[4,4096]{1,0:T(4,128)S(1)} collective-permute-done((f32[4,4096]{1,0:T(4,128)S(1)}, f32[4,4096]{1,0:T(4,128)S(1)}, u32[]{:S(2)}, u32[]{:S(2)}) %collective-permute-start.3) | collective-permute-done | bytes 65568 | tf_op jit(solution)/shard_map/ppermute | solution.py:21
  38.2 2.5 bitcast_dynamic-update-slice_fusion.6
  40.8 2.2 multiply_add_fusion.4
  43.0 5.1 %collective-permute-start.4 = (f32[8,4096]{1,0:T(8,128)S(1)}, f32[8,4096]{1,0:T(8,128)S(1)}, u32[]{:S(2)}, u32[]{:S(2)}) collective-permute-start(f32[8,4096]{1,0:T(8,128)S(1)} %get-tuple-element.33), channel_id=1, source_target_pairs={{0,1},{1,2},{2,3},{3,4},{4,5},{5,6},{6,7},{8,9},{9,10},{10,11},{11... | collective-permute-start | bytes 393224 | tf_op jit(solution)/shard_map/ppermute | solution.py:20
  48.2 1.5 collective-permute-start.5
  49.6 1.0 collective-permute-done.4
  50.7 4.4 %collective-permute-done.5 = f32[8,4096]{1,0:T(8,128)S(1)} collective-permute-done((f32[8,4096]{1,0:T(8,128)S(1)}, f32[8,4096]{1,0:T(8,128)S(1)}, u32[]{:S(2)}, u32[]{:S(2)}) %collective-permute-start.5) | collective-permute-done | bytes 131104 | tf_op jit(solution)/shard_map/ppermute | solution.py:21
  55.0 2.4 bitcast_dynamic-update-slice_fusion.5
  57.4 2.2 multiply_add_fusion.3
  59.7 3.9 %collective-permute-start.6 = (f32[16,4096]{1,0:T(8,128)S(1)}, f32[16,4096]{1,0:T(8,128)S(1)}, u32[]{:S(2)}, u32[]{:S(2)}) collective-permute-start(f32[16,4096]{1,0:T(8,128)S(1)} %get-tuple-element.31), channel_id=1, source_target_pairs={{0,1},{1,2},{2,3},{3,4},{4,5},{5,6},{6,7},{8,9},{9,10},{10,11},{11... | collective-permute-start | bytes 786440 | tf_op jit(solution)/shard_map/ppermute | solution.py:20
  63.6 1.3 collective-permute-start.7
  64.9 2.6 collective-permute-done.6
  67.4 4.4 %collective-permute-done.7 = f32[16,4096]{1,0:T(8,128)S(1)} collective-permute-done((f32[16,4096]{1,0:T(8,128)S(1)}, f32[16,4096]{1,0:T(8,128)S(1)}, u32[]{:S(2)}, u32[]{:S(2)}) %collective-permute-start.7) | collective-permute-done | bytes 262176 | tf_op jit(solution)/shard_map/ppermute | solution.py:21
  71.9 2.6 bitcast_dynamic-update-slice_fusion.4
  74.4 2.2 multiply_add_fusion.2
  76.7 0.1 fusion.88
  76.7 3.1 %collective-permute-start.8 = (f32[32,4096]{1,0:T(8,128)S(1)}, f32[32,4096]{1,0:T(8,128)S(1)}, u32[]{:S(2)}, u32[]{:S(2)}) collective-permute-start(f32[32,4096]{1,0:T(8,128)S(1)} %get-tuple-element.29), channel_id=1, source_target_pairs={{0,1},{1,2},{2,3},{3,4},{4,5},{5,6},{6,7},{8,9},{9,10},{10,11},{11... | collective-permute-start | bytes 1572872 | tf_op jit(solution)/shard_map/ppermute | solution.py:20
  79.9 1.3 collective-permute-start.9
  81.2 5.3 %collective-permute-done.8 = f32[32,4096]{1,0:T(8,128)S(1)} collective-permute-done((f32[32,4096]{1,0:T(8,128)S(1)}, f32[32,4096]{1,0:T(8,128)S(1)}, u32[]{:S(2)}, u32[]{:S(2)}) %collective-permute-start.8) | collective-permute-done | bytes 524320 | tf_op jit(solution)/shard_map/ppermute | solution.py:20
  86.5 4.4 %collective-permute-done.9 = f32[32,4096]{1,0:T(8,128)S(1)} collective-permute-done((f32[32,4096]{1,0:T(8,128)S(1)}, f32[32,4096]{1,0:T(8,128)S(1)}, u32[]{:S(2)}, u32[]{:S(2)}) %collective-permute-start.9) | collective-permute-done | bytes 524320 | tf_op jit(solution)/shard_map/ppermute | solution.py:21
  91.0 2.3 bitcast_dynamic-update-slice_fusion.3
  93.3 2.2 multiply_add_fusion.1
  95.5 0.2 fusion.87
  95.7 3.2 %collective-permute-start.10 = (f32[64,4096]{1,0:T(8,128)S(1)}, f32[64,4096]{1,0:T(8,128)S(1)}, u32[]{:S(2)}, u32[]{:S(2)}) collective-permute-start(f32[64,4096]{1,0:T(8,128)S(1)} %get-tuple-element.27), channel_id=1, source_target_pairs={{0,1},{1,2},{2,3},{3,4},{4,5},{5,6},{6,7},{8,9},{9,10},{10,11},{11... | collective-permute-start | bytes 3145736 | tf_op jit(solution)/shard_map/ppermute | solution.py:20
  98.9 1.3 collective-permute-start.11
  100.2 15.0 %collective-permute-done.10 = f32[64,4096]{1,0:T(8,128)S(1)} collective-permute-done((f32[64,4096]{1,0:T(8,128)S(1)}, f32[64,4096]{1,0:T(8,128)S(1)}, u32[]{:S(2)}, u32[]{:S(2)}) %collective-permute-start.10) | collective-permute-done | bytes 1048608 | tf_op jit(solution)/shard_map/ppermute | solution.py:20
  115.2 4.2 %collective-permute-done.11 = f32[64,4096]{1,0:T(8,128)S(1)} collective-permute-done((f32[64,4096]{1,0:T(8,128)S(1)}, f32[64,4096]{1,0:T(8,128)S(1)}, u32[]{:S(2)}, u32[]{:S(2)}) %collective-permute-start.11) | collective-permute-done | bytes 1048608 | tf_op jit(solution)/shard_map/ppermute | solution.py:21
  119.4 2.2 bitcast_dynamic-update-slice_fusion.2
  121.6 1.1 multiply_add_fusion
  122.8 1.3 collective-permute-start.13
  124.1 4.9 %collective-permute-start.12 = (f32[128,4096]{1,0:T(8,128)S(1)}, f32[128,4096]{1,0:T(8,128)S(1)}, u32[]{:S(2)}, u32[]{:S(2)}) collective-permute-start(f32[128,4096]{1,0:T(8,128)S(1)} %multiply_add_fusion), channel_id=1, source_target_pairs={{0,1},{1,2},{2,3},{3,4},{4,5},{5,6},{6,7},{8,9},{9,10},{10,11},{11... | collective-permute-start | bytes 6291464 | tf_op jit(solution)/shard_map/ppermute | solution.py:20
  129.0 35.9 %collective-permute-done.13 = f32[128,4096]{1,0:T(8,128)S(1)} collective-permute-done((f32[128,4096]{1,0:T(8,128)S(1)}, f32[128,4096]{1,0:T(8,128)S(1)}, u32[]{:S(2)}, u32[]{:S(2)}) %collective-permute-start.13) | collective-permute-done | bytes 2097184 | tf_op jit(solution)/shard_map/ppermute | solution.py:21
  164.8 1.2 collective-permute-done.12
  166.0 3.8 %multiply_reduce_fusion = (f32[]{:T(128)}, f32[]{:T(128)}, f32[]{:T(128)}, f32[]{:T(128)}, f32[]{:T(128)}, /*index=5*/f32[]{:T(128)}, f32[]{:T(128)}, f32[]{:T(128)}, f32[128,4096]{1,0:T(8,128)S(1)}) fusion(f32[128,4096]{1,0:T(8,128)S(1)} %get-tuple-element.16, f32[128,4096]{1,0:T(8,128)S(1)} %get-tuple-element.18, f32[128,4096]{1,0:T(8,128)S(1)} %get-tuple-element.20, ...), kind=kLoop, calls=%fused_computation.142 | loop fusion | flops 17825784 | bytes 23068704 | tf_op jit(solution)/shard_map/reduce_sum | solution.py:74
  169.8 1.6 bitcast_dynamic-update-slice_fusion.1
  171.5 1.5 bitcast_dynamic-update-slice_fusion
  173.0 0.0 reduce-scatter.2.cloned.1.call-update
  173.0 5.2 %stack.74 = f32[8]{0:T(128)S(1)} concatenate(f32[1]{0:T(128)} %bitcast.10, f32[1]{0:T(128)} %bitcast.11, f32[1]{0:T(128)} %bitcast.12, f32[1]{0:T(128)} %bitcast.13, f32[1]{0:T(128)} %bitcast.14, f32[1]{0:T(128)} %bitcast.15, f32[1]{0:T(128)} %bitcast.16, f32[1]{0:T(128)} %bitcast.17), dimensions={0} | concatenate | bytes 64 | tf_op jit(solution)/shard_map/stack | solution.py:75
  178.2 17.6 %all-reduce.7 = (f32[1,8]{1,0:T(1,128)S(1)}, f32[1]{0:T(128)}) all-reduce(f32[1,8]{1,0:T(1,128)S(1)} %bitcast.33, f32[1]{0:T(128)} %bitcast.19), channel_id=1, replica_groups=mesh['mem'=32,'row'=8] {'row'}, use_global_device_ids=true, to_apply=%region_9.10 | all-reduce | flops 9 | bytes 72 | tf_op jit(solution)/shard_map/psum | solution.py:77
  197.1 0.5 subtract_bitcast_fusion
  197.6 101.3 %reduce-scatter.2.cloned.1.call-done = f32[1,8,128,128]{3,2,1,0:T(8,128)} async-done(((f32[1,8,128,4096]{3,2,1,0:T(8,128)}), f32[1,8,128,128]{3,2,1,0:T(8,128)}) %reduce-scatter.2.cloned.1.call-update) | async-done | bytes 524304 | tf_op jit(solution)/shard_map/reduce_scatter | solution.py:83
  299.0 1.9 broadcast_multiply_fusion
  (4 shorter events, 0.1 us)
Async XLA Ops:
  7.2 2.9 copy-start
  7.2 291.8 %reduce-scatter.2.cloned.1.call-start = ((), (), s32[]{:S(2)}) async-start(), calls=%async_computation.1 | async-start | bytes 17301504 | tf_op jit(solution)/shard_map/reduce_scatter | solution.py:83
  12.7 5.4 %collective-permute-start = (f32[2,4096]{1,0:T(2,128)S(1)}, f32[2,4096]{1,0:T(2,128)S(1)}, u32[]{:S(2)}, u32[]{:S(2)}) collective-permute-start(f32[2,4096]{1,0:T(2,128)S(1)} %get-tuple-element.37), channel_id=1, source_target_pairs={{0,1},{1,2},{2,3},{3,4},{4,5},{5,6},{6,7},{8,9},{9,10},{10,11},{11... | collective-permute-start | bytes 98312 | tf_op jit(solution)/shard_map/ppermute | solution.py:20
  16.5 5.8 %collective-permute-start.1 = (f32[2,4096]{1,0:T(2,128)S(1)}, f32[2,4096]{1,0:T(2,128)S(1)}, u32[]{:S(2)}, u32[]{:S(2)}) collective-permute-start(f32[2,4096]{1,0:T(2,128)S(1)} %get-tuple-element.38), channel_id=1, source_target_pairs={{1,0},{2,1},{3,2},{4,3},{5,4},{6,5},{7,6},{9,8},{10,9},{11,10},{12... | collective-permute-start | bytes 98312 | tf_op jit(solution)/shard_map/ppermute | solution.py:21
  27.2 5.7 %collective-permute-start.2 = (f32[4,4096]{1,0:T(4,128)S(1)}, f32[4,4096]{1,0:T(4,128)S(1)}, u32[]{:S(2)}, u32[]{:S(2)}) collective-permute-start(f32[4,4096]{1,0:T(4,128)S(1)} %get-tuple-element.35), channel_id=1, source_target_pairs={{0,1},{1,2},{2,3},{3,4},{4,5},{5,6},{6,7},{8,9},{9,10},{10,11},{11... | collective-permute-start | bytes 196616 | tf_op jit(solution)/shard_map/ppermute | solution.py:20
  31.0 7.2 %collective-permute-start.3 = (f32[4,4096]{1,0:T(4,128)S(1)}, f32[4,4096]{1,0:T(4,128)S(1)}, u32[]{:S(2)}, u32[]{:S(2)}) collective-permute-start(f32[4,4096]{1,0:T(4,128)S(1)} %get-tuple-element.36), channel_id=1, source_target_pairs={{1,0},{2,1},{3,2},{4,3},{5,4},{6,5},{7,6},{9,8},{10,9},{11,10},{12... | collective-permute-start | bytes 196616 | tf_op jit(solution)/shard_map/ppermute | solution.py:21
  43.0 7.6 %collective-permute-start.4 = (f32[8,4096]{1,0:T(8,128)S(1)}, f32[8,4096]{1,0:T(8,128)S(1)}, u32[]{:S(2)}, u32[]{:S(2)}) collective-permute-start(f32[8,4096]{1,0:T(8,128)S(1)} %get-tuple-element.33), channel_id=1, source_target_pairs={{0,1},{1,2},{2,3},{3,4},{4,5},{5,6},{6,7},{8,9},{9,10},{10,11},{11... | collective-permute-start | bytes 393224 | tf_op jit(solution)/shard_map/ppermute | solution.py:20
  48.2 6.9 %collective-permute-start.5 = (f32[8,4096]{1,0:T(8,128)S(1)}, f32[8,4096]{1,0:T(8,128)S(1)}, u32[]{:S(2)}, u32[]{:S(2)}) collective-permute-start(f32[8,4096]{1,0:T(8,128)S(1)} %get-tuple-element.34), channel_id=1, source_target_pairs={{1,0},{2,1},{3,2},{4,3},{5,4},{6,5},{7,6},{9,8},{10,9},{11,10},{12... | collective-permute-start | bytes 393224 | tf_op jit(solution)/shard_map/ppermute | solution.py:21
  59.7 7.8 %collective-permute-start.6 = (f32[16,4096]{1,0:T(8,128)S(1)}, f32[16,4096]{1,0:T(8,128)S(1)}, u32[]{:S(2)}, u32[]{:S(2)}) collective-permute-start(f32[16,4096]{1,0:T(8,128)S(1)} %get-tuple-element.31), channel_id=1, source_target_pairs={{0,1},{1,2},{2,3},{3,4},{4,5},{5,6},{6,7},{8,9},{9,10},{10,11},{11... | collective-permute-start | bytes 786440 | tf_op jit(solution)/shard_map/ppermute | solution.py:20
  63.6 8.3 %collective-permute-start.7 = (f32[16,4096]{1,0:T(8,128)S(1)}, f32[16,4096]{1,0:T(8,128)S(1)}, u32[]{:S(2)}, u32[]{:S(2)}) collective-permute-start(f32[16,4096]{1,0:T(8,128)S(1)} %get-tuple-element.32), channel_id=1, source_target_pairs={{1,0},{2,1},{3,2},{4,3},{5,4},{6,5},{7,6},{9,8},{10,9},{11,10},{12... | collective-permute-start | bytes 786440 | tf_op jit(solution)/shard_map/ppermute | solution.py:21
  76.7 9.8 %collective-permute-start.8 = (f32[32,4096]{1,0:T(8,128)S(1)}, f32[32,4096]{1,0:T(8,128)S(1)}, u32[]{:S(2)}, u32[]{:S(2)}) collective-permute-start(f32[32,4096]{1,0:T(8,128)S(1)} %get-tuple-element.29), channel_id=1, source_target_pairs={{0,1},{1,2},{2,3},{3,4},{4,5},{5,6},{6,7},{8,9},{9,10},{10,11},{11... | collective-permute-start | bytes 1572872 | tf_op jit(solution)/shard_map/ppermute | solution.py:20
  79.9 11.1 %collective-permute-start.9 = (f32[32,4096]{1,0:T(8,128)S(1)}, f32[32,4096]{1,0:T(8,128)S(1)}, u32[]{:S(2)}, u32[]{:S(2)}) collective-permute-start(f32[32,4096]{1,0:T(8,128)S(1)} %get-tuple-element.30), channel_id=1, source_target_pairs={{1,0},{2,1},{3,2},{4,3},{5,4},{6,5},{7,6},{9,8},{10,9},{11,10},{12... | collective-permute-start | bytes 1572872 | tf_op jit(solution)/shard_map/ppermute | solution.py:21
  95.7 19.5 %collective-permute-start.10 = (f32[64,4096]{1,0:T(8,128)S(1)}, f32[64,4096]{1,0:T(8,128)S(1)}, u32[]{:S(2)}, u32[]{:S(2)}) collective-permute-start(f32[64,4096]{1,0:T(8,128)S(1)} %get-tuple-element.27), channel_id=1, source_target_pairs={{0,1},{1,2},{2,3},{3,4},{4,5},{5,6},{6,7},{8,9},{9,10},{10,11},{11... | collective-permute-start | bytes 3145736 | tf_op jit(solution)/shard_map/ppermute | solution.py:20
  98.9 20.5 %collective-permute-start.11 = (f32[64,4096]{1,0:T(8,128)S(1)}, f32[64,4096]{1,0:T(8,128)S(1)}, u32[]{:S(2)}, u32[]{:S(2)}) collective-permute-start(f32[64,4096]{1,0:T(8,128)S(1)} %get-tuple-element.28), channel_id=1, source_target_pairs={{1,0},{2,1},{3,2},{4,3},{5,4},{6,5},{7,6},{9,8},{10,9},{11,10},{12... | collective-permute-start | bytes 3145736 | tf_op jit(solution)/shard_map/ppermute | solution.py:21
  122.8 42.1 %collective-permute-start.13 = (f32[128,4096]{1,0:T(8,128)S(1)}, f32[128,4096]{1,0:T(8,128)S(1)}, u32[]{:S(2)}, u32[]{:S(2)}) collective-permute-start(f32[128,4096]{1,0:T(8,128)S(1)} %multiply_add_fusion), channel_id=1, source_target_pairs={{1,0},{2,1},{3,2},{4,3},{5,4},{6,5},{7,6},{9,8},{10,9},{11,10},{12... | collective-permute-start | bytes 6291464 | tf_op jit(solution)/shard_map/ppermute | solution.py:21
  124.1 41.9 %collective-permute-start.12 = (f32[128,4096]{1,0:T(8,128)S(1)}, f32[128,4096]{1,0:T(8,128)S(1)}, u32[]{:S(2)}, u32[]{:S(2)}) collective-permute-start(f32[128,4096]{1,0:T(8,128)S(1)} %multiply_add_fusion), channel_id=1, source_target_pairs={{0,1},{1,2},{2,3},{3,4},{4,5},{5,6},{6,7},{8,9},{9,10},{10,11},{11... | collective-permute-start | bytes 6291464 | tf_op jit(solution)/shard_map/ppermute | solution.py:20
Sparse Core Ops, SparseCore 0:
  173.1 125.8 reduce-scatter.1
where the time goes:
time: 308 us
  waiting for transfers between devices  190 us (62%)
  other arithmetic  41.7 us (14%)
  starting transfers between devices  37.2 us (12%)
  blocking collectives  17.6 us (6%)
  between operations  15.5 us (5%)
  local copies, waits for them, and re-layouts  5.59 us (2%)
    reduce_scatter x1, waiting for transfers between devices, on_device(): summed = lax.psum_scatter(stacked, 'mem', scatter_dimension=3, tiled=True)  101 us
    ppermute x7, waiting for transfers between devices, extended(): after = lax.ppermute(first, axis, down)  62.8 us
    ppermute x7, starting transfers between devices, extended(): before = lax.ppermute(last, axis, up)  27.9 us
    ppermute x7, waiting for transfers between devices, extended(): before = lax.ppermute(last, axis, up)  26 us
    psum x1, blocking collectives, on_device(): sum_totals, sum_counts = lax.psum((local_totals, local_counts), 'row')  17.6 us
    unnamed x7, other arithmetic  16.2 us
    add x7, other arithmetic, column_pass(): result + KERNEL[index] * padded[:, index * spacing:index * spacing + brea...  14.5 us
    ppermute x7, starting transfers between devices, extended(): after = lax.ppermute(first, axis, down)  9.23 us
  transfers between devices with their start and end apart: 15, of which 15 were waited for; matrix products, arithmetic and copies ran while one was open for 2% of the time, Pallas kernels for 0%

commit v1 on v0

v1 whole, which is shorter than its diff:
```python
import functools

import jax
import jax.numpy as jnp
from jax import lax
from jax.experimental import pallas as pl
from jax.experimental.pallas import tpu as pltpu
from jax.sharding import PartitionSpec as P

MESH = pl.DeviceIdType.MESH
F32, BF16 = jnp.float32, jnp.bfloat16

LEVELS = 7
H = 128
W = 4096
TILE = 256
TILES = W // TILE
SIDE = 4
ROWS = 8
MEMBERS = 32
TAPS = (1.0 / 16.0, 4.0 / 16.0, 6.0 / 16.0, 4.0 / 16.0, 1.0 / 16.0)
WEIGHTS = [4.0 ** min(k + 1, LEVELS) for k in range(LEVELS + 1)]
PAD = 128

SLOT_ROW = (128, 384, 0, 512)
HALO = (
    (0, 1, 112, 16),
    (1, -1, 0, 16),
    (0, 1, 64, 48),
    (1, -1, 16, 48),
    (0, 1, 0, 64),
    (1, -1, 64, 64),
    (2, 2, 32, 96),
    (3, -2, 0, 96),
    (2, 2, 0, 32),
    (3, -2, 96, 32),
)
PIECES = [[(k, 0), (k, 32), (k, 64), (k, 96)] for k in range(6)]
PIECES += [[(6, 32), (6, 64), (7, 32), (7, 64)], [(6, 0), (6, 96), (7, 0), (7, 96)]]
BLOCK = 32


def kernel(
    e_ref, obs_ref, out_ref, skill_ref,
    halo, ext, ub, sb, part, pair, ring1, ring2, xr, rm, rm7, xe, xi, ci, ce, obuf, acc, peers,
    osem, zsend, zrecv, psend, precv, ksend, krecv,
):
    mem, row = lax.axis_index("mem"), lax.axis_index("row")
    c, y, x = lax.rem(mem, 2), lax.rem(mem // 2, SIDE), mem // (2 * SIDE)

    def at(xx, yy, cc):
        return (xx * SIDE + yy) * 2 + cc

    def along_z(step):
        return (mem, lax.rem(row + step + ROWS, ROWS))

    def along(axis, step):
        if axis == "y":
            return (at(x, lax.rem(y + step + SIDE, SIDE), c), row)
        return (at(lax.rem(x + step + SIDE, SIDE), y, c), row)

    sibling = (at(x, y, 1 - c), row)

    barrier = pltpu.get_barrier_semaphore()
    partners = [along_z(d) for d in range(1, ROWS)] + [sibling]
    partners += [along(axis, d) for axis in "xy" for d in (1, -1)]
    for partner in partners:
        pl.semaphore_signal(barrier, inc=1, device_id=partner, device_id_type=MESH)
    pl.semaphore_wait(barrier, len(partners))

    sends = []

    def remote(src, dst, send, recv, target):
        copy = pltpu.make_async_remote_copy(
            src_ref=src, dst_ref=dst, send_sem=send, recv_sem=recv, device_id=target, device_id_type=MESH
        )
        copy.start()
        sends.append(copy)
        return copy

    halos = []
    for n, (slot, step, first, rows) in enumerate(HALO):
        span = pl.ds(first, rows)
        halos.append(remote(e_ref.at[span, :], halo.at[slot, span, :], zsend.at[n], zrecv.at[n], along_z(step)))

    def take(n):
        slot, _, first, rows = HALO[n]
        halos[n].wait_recv()

        @pl.loop(0, W // 512)
        def _(i):
            lanes = pl.ds(pl.multiple_of(i * 512, 512), 512)
            ext[SLOT_ROW[slot] + first : SLOT_ROW[slot] + first + rows, lanes] = halo[
                slot, first : first + rows, lanes
            ].astype(BF16)

    @pl.loop(0, W // 512)
    def _(i):
        lanes = pl.ds(pl.multiple_of(i * 512, 512), 512)
        ext[256:384, lanes] = e_ref[:, lanes].astype(BF16)
        for first, rows in ((0, 32), (128, 128), (384, 128), (608, 32)):
            ext[first : first + rows, lanes] = jnp.zeros((rows, 512), BF16)

    acc[...] = jnp.zeros_like(acc)

    def taps(load, spacing):
        a, b, m, d, e = (load((q - 2) * spacing) for q in range(5))
        return TAPS[0] * (a + e) + TAPS[1] * (b + d) + TAPS[2] * m

    def split(value):
        high = value.astype(BF16)
        return high, (value - high.astype(F32)).astype(BF16)

    for side in range(2):
        xr[side, 0:PAD, :] = jnp.zeros((PAD, 128), F32)
        xr[side, PAD + 640 : 2 * PAD + 640, :] = jnp.zeros((PAD, 128), F32)
    for lane_block in range(5):
        index = lax.broadcasted_iota(jnp.int32, (640, 128), 0)
        domain = index + (row * H - 256)
        inside = (domain >= 0) & (domain < ROWS * H)
        lane = lax.broadcasted_iota(jnp.int32, (640, 128), 1) + lane_block * 128
        xr[0, PAD : PAD + 640, :] = jnp.where(inside & (index == lane), 1.0, 0.0)
        for level in range(1, LEVELS + 1):
            src, dst = (level + 1) % 2, level % 2
            new = taps(lambda o: xr[src, PAD + o : PAD + o + 640, :], 2 ** (level - 1))
            xr[dst, PAD : PAD + 640, :] = jnp.where(inside, new, 0.0)
            high, low = split(xr[dst, PAD + 256 : PAD + 384, :])
            if level == LEVELS:
                rm7[0:H, lane_block * 128 : lane_block * 128 + 128] = high
                rm7[H : 2 * H, lane_block * 128 : lane_block * 128 + 128] = low
            elif 1 <= lane_block <= 3:
                rm[level - 1, 0:H, lane_block * 128 - 128 : lane_block * 128] = high
                rm[level - 1, H : 2 * H, lane_block * 128 - 128 : lane_block * 128] = low

    for side in range(2):
        for start in (0, PAD + 768):
            xi[side, start : start + PAD, :] = jnp.zeros((PAD, TILE), F32)
        for start in (0, PAD + 512):
            xe[side, start : start + PAD, :] = jnp.zeros((PAD, 512), F32)
    xi[0, PAD : PAD + 768, :] = jnp.where(
        lax.broadcasted_iota(jnp.int32, (768, TILE), 0) - 256 == lax.broadcasted_iota(jnp.int32, (768, TILE), 1),
        1.0, 0.0,
    )
    xe[0, PAD : PAD + 512, :] = jnp.where(
        lax.broadcasted_iota(jnp.int32, (512, 512), 0) == lax.broadcasted_iota(jnp.int32, (512, 512), 1), 1.0, 0.0
    )

    def column_operators(level):
        src, dst = (level + 1) % 2, level % 2
        spacing = 2 ** (level - 1)

        @pl.loop(0, TILE // 128)
        def _(i):
            lanes = pl.ds(pl.multiple_of(i * 128, 128), 128)
            new = taps(lambda o: xi[src, PAD + o : PAD + o + 768, lanes], spacing)
            xi[dst, PAD : PAD + 768, lanes] = new
            ci[0, :, lanes], ci[1, :, lanes] = split(new)

        @pl.loop(0, 512 // 128)
        def _(i):
            lanes = pl.ds(pl.multiple_of(i * 128, 128), 128)
            new = taps(lambda o: xe[src, PAD + o : PAD + o + 512, lanes], spacing)
            xe[dst, PAD : PAD + 512, lanes] = new
            ce[0, :, lanes], ce[1, :, lanes] = split(new)

    def level_pass(level, spans):
        reach = 256 if level == LEVELS else 128
        height = sum(rows for _, rows in spans)
        ops = rm7 if level == LEVELS else rm.at[level - 1]
        depth = slice(0, 640) if level == LEVELS else slice(128, 512)

        def pick(ref, offset):
            return [ref[offset + first : offset + first + rows, :] for first, rows in spans]

        @pl.loop(0, TILES)
        def _(t):
            lanes = pl.ds(pl.multiple_of(t * TILE, TILE), TILE)
            left = jnp.concatenate(pick(ops, 0) + pick(ops, H), axis=0)
            both = jnp.dot(left, ext[depth, lanes], preferred_element_type=F32)
            high, low = split(both[:height] + both[height:])
            done = 0
            for first, rows in spans:
                ub[t, first : first + rows, :] = high[done : done + rows]
                ub[t, H + first : H + first + rows, :] = low[done : done + rows]
                done += rows

        def finish(t, both, cross):
            smooth = both[:height] + both[height:] + cross
            lanes = pl.ds(pl.multiple_of(t * TILE, TILE), TILE) if not isinstance(t, int) else pl.ds(t * TILE, TILE)
            done = 0
            for first, rows in spans:
                now = smooth[done : done + rows]
                before = e_ref[first : first + rows, lanes] if level == 1 else sb[t, first : first + rows, :]
                store(level - 1, t, first, rows, before - now)
                if level == LEVELS:
                    store(LEVELS, t, first, rows, now)
                else:
                    sb[t, first : first + rows, :] = now
                done += rows

        def store(k, t, first, rows, component):
            energy = component * component * (WEIGHTS[k] / MEMBERS)
            for core in range(2):
                part[k, core, t // SIDE, t % SIDE, first : first + rows, :] = energy[:, core * 128 : core * 128 + 128]
            folded = energy[:, 0:128] + energy[:, 128:256]
            acc[k] += jnp.sum(folded.reshape(rows // 8, 8, 128), axis=0)

        def lhs(tiles):
            return jnp.concatenate(
                [
                    jnp.concatenate(
                        [ub[t, offset + first : offset + first + rows, lanes] for t, lanes in tiles], axis=1
                    )
                    for offset in (0, H)
                    for first, rows in spans
                ],
                axis=0,
            )

        near_left, whole, near_right = slice(256 - reach, 256), slice(0, 256), slice(0, reach)

        @pl.loop(1, TILES - 1)
        def _(t):
            left = lhs([(t - 1, near_left), (t, whole), (t + 1, near_right)])
            depth = slice(256 - reach, 512 + reach)
            both = jnp.dot(left, ci[0, depth, :], preferred_element_type=F32)
            cross = jnp.dot(left[:height], ci[1, depth, :], preferred_element_type=F32)
            finish(t, both, cross)

        for t, tiles, out, depth in (
            (0, [(0, whole), (1, near_right)], slice(0, 256), slice(0, 256 + reach)),
            (TILES - 1, [(TILES - 2, near_left), (TILES - 1, whole)], slice(256, 512), slice(256 - reach, 512)),
        ):
            left = lhs(tiles)
            dims = (((1,), (1,)), ((), ()))
            both = lax.dot_general(left, ce[0, out, depth], dims, preferred_element_type=F32)
            cross = lax.dot_general(left[:height], ce[1, out, depth], dims, preferred_element_type=F32)
            finish(t, both, cross)

    flights = {}

    def block_of(p, i, axis, pos, stage):
        k, first = PIECES[p][i]
        rows = pl.ds(first, BLOCK)
        if stage == 1:
            if axis == "y":
                return part.at[k, c, :, pos, rows, :]
            return part.at[k, c, pos, :, rows, :]
        if axis == "y":
            return part.at[k, c, x, pos, rows, :]
        return part.at[k, c, pos, y, rows, :]

    def axis_of(half, stage):
        return "yx"[(half + stage - 1) % 2]

    def spot(axis, step):
        return lax.rem((y if axis == "y" else x) + step + SIDE, SIDE)

    def pair_start(p):
        for i, (k, first) in enumerate(PIECES[p]):
            rows = pl.ds(first, BLOCK)
            flights[p, 0, i] = remote(
                part.at[k, 1 - c, :, :, rows, :], pair.at[k, :, :, rows, :], psend.at[p, i], precv.at[p, i], sibling
            )

    def ring_copy(p, stage, half, n, i, pos, step):
        axis = axis_of(half, stage)
        landing = (ring1 if stage == 1 else ring2).at[p, half, n]
        sem = 4 + (stage - 1) * 12 + half * 6 + n
        flights[p, stage, half, n] = remote(
            block_of(p, i, axis, spot(axis, pos), stage), landing, psend.at[p, sem], precv.at[p, sem], along(axis, step)
        )

    def ring_start(p, stage):
        for half in range(2):
            i0, i1 = 2 * half, 2 * half + 1
            ring_copy(p, stage, half, 0, i0, 2, 1)
            ring_copy(p, stage, half, 1, i1, 2, -1)
            ring_copy(p, stage, half, 2, i1, 1, 1)
            ring_copy(p, stage, half, 3, i0, -1, -1)

    def ring_add(p, stage, half, n, i, pos):
        axis = axis_of(half, stage)
        flights[p, stage, half, n].wait_recv()
        block = block_of(p, i, axis, spot(axis, pos), stage)
        block[...] = block[...] + (ring1 if stage == 1 else ring2)[p, half, n]

    def ring_middle(p, stage):
        for half in range(2):
            i0, i1 = 2 * half, 2 * half + 1
            ring_add(p, stage, half, 0, i0, 1)
            ring_copy(p, stage, half, 4, i0, 1, 1)
            ring_add(p, stage, half, 1, i1, -1)
            ring_copy(p, stage, half, 5, i1, -1, -1)

    def ring_end(p, stage):
        for half in range(2):
            i0, i1 = 2 * half, 2 * half + 1
            ring_add(p, stage, half, 3, i0, 0)
            ring_add(p, stage, half, 2, i1, 0)
            ring_add(p, stage, half, 4, i0, 0)
            ring_add(p, stage, half, 5, i1, 0)

    def advance(p, step):
        if step == 0:
            pair_start(p)
        elif step == 1:
            for i, (k, first) in enumerate(PIECES[p]):
                flights[p, 0, i].wait_recv()

                @pl.loop(0, SIDE)
                def _(j):
                    rows = pl.ds(first, BLOCK)
                    part[k, c, j, :, rows, :] = part[k, c, j, :, rows, :] + pair[k, j, :, rows, :]

            ring_start(p, 1)
        elif step == 2:
            ring_middle(p, 1)
        elif step == 3:
            ring_end(p, 1)
            ring_start(p, 2)
        elif step == 4:
            ring_middle(p, 2)
        elif step == 5:
            ring_end(p, 2)
            for k, first in PIECES[p]:
                out_ref[k, first : first + BLOCK, :] = part[k, c, x, y, pl.ds(first, BLOCK), :]

    position = {}

    def tick(limit):
        for p in sorted(position):
            if p <= limit and position[p] < 5:
                position[p] += 1
                advance(p, position[p])

    def begin(p):
        position[p] = 0
        advance(p, 0)

    everything = [(0, H)]
    for level in range(1, LEVELS):
        column_operators(level)
        if level == 1:
            take(0), take(1)
        if level == 4:
            take(2), take(3)
        if level == 6:
            take(4), take(5)
        level_pass(level, everything)
        tick(level - 2)
        begin(level - 1)

    @pl.loop(0, W // 512)
    def _(i):
        copy = pltpu.make_async_copy(obs_ref.at[:, pl.ds(pl.multiple_of(i * 512, 512), 512)], obuf, osem)
        copy.start()
        copy.wait()
        seen = jnp.where(obuf[...] > 0, 1.0, 0.0)
        acc[LEVELS + 1] += jnp.sum(jnp.sum(seen.reshape(16, 8, 4, 128), axis=0), axis=1)

    column_operators(LEVELS)
    while any(position[p] < 5 for p in range(6)):
        tick(5)

    take(6), take(7)
    level_pass(LEVELS, [(32, 64)])
    begin(6)
    tick(6)
    tick(6)
    take(8), take(9)
    level_pass(LEVELS, [(0, 32), (96, 32)])
    begin(7)

    tallies = [
        remote(acc, peers.at[d - 1], ksend.at[d - 1], krecv.at[d - 1], along_z(d)) for d in range(1, ROWS)
    ]
    while any(position[p] < 5 for p in position):
        tick(7)

    for copy in tallies:
        copy.wait_recv()
    cells = float(ROWS * H * W)

    def total(k):
        value = acc[k]
        for d in range(ROWS - 1):
            value = value + peers[d, k]
        return jnp.sum(jnp.sum(value, axis=0, keepdims=True), axis=1, keepdims=True)

    base_rate = total(LEVELS + 1) / cells
    spread = 2.0 * base_rate * (1.0 - base_rate)
    lane = lax.broadcasted_iota(jnp.int32, (1, 8), 1)
    result = jnp.zeros((1, 8), F32)
    for k in range(LEVELS + 1):
        mean_error = total(k) * (MEMBERS / WEIGHTS[k]) / cells
        result = jnp.where(lane == k, 1.0 - mean_error * (LEVELS + 1) / spread, result)
    skill_ref[...] = result

    for copy in sends:
        copy.wait_send()


def on_device(predicted_surpass_tally, observed_surpass_tally):
    error = (predicted_surpass_tally[0] > 0).astype(F32) - (observed_surpass_tally > 0).astype(F32)
    vmem = pl.BlockSpec(memory_space=pltpu.VMEM)
    energy, skill = pl.pallas_call(
        kernel,
        out_shape=(
            jax.ShapeDtypeStruct((LEVELS + 1, H, 128), F32),
            jax.ShapeDtypeStruct((1, LEVELS + 1), F32),
        ),
        in_specs=[vmem, pl.BlockSpec(memory_space=pl.ANY)],
        out_specs=(vmem, vmem),
        scratch_shapes=[
            pltpu.VMEM((4, H, W), F32),
            pltpu.VMEM((5 * H, W), BF16),
            pltpu.VMEM((TILES, 2 * H, TILE), BF16),
            pltpu.VMEM((TILES, H, TILE), F32),
            pltpu.VMEM((LEVELS + 1, 2, SIDE, SIDE, H, 128), F32),
            pltpu.VMEM((LEVELS + 1, SIDE, SIDE, H, 128), F32),
            pltpu.VMEM((len(PIECES), 2, 6, SIDE, BLOCK, 128), F32),
            pltpu.VMEM((len(PIECES), 2, 6, BLOCK, 128), F32),
            pltpu.VMEM((2, 640 + 2 * PAD, 128), F32),
            pltpu.VMEM((LEVELS - 1, 2 * H, 384), BF16),
            pltpu.VMEM((2 * H, 640), BF16),
            pltpu.VMEM((2, 512 + 2 * PAD, 512), F32),
            pltpu.VMEM((2, 768 + 2 * PAD, TILE), F32),
            pltpu.VMEM((2, 768, TILE), BF16),
            pltpu.VMEM((2, 512, 512), BF16),
            pltpu.VMEM((H, 512), jnp.int32),
            pltpu.VMEM((LEVELS + 2, 8, 128), F32),
            pltpu.VMEM((ROWS - 1, LEVELS + 2, 8, 128), F32),
            pltpu.SemaphoreType.DMA,
            pltpu.SemaphoreType.DMA((len(HALO),)),
            pltpu.SemaphoreType.DMA((len(HALO),)),
            pltpu.SemaphoreType.DMA((len(PIECES), 28)),
            pltpu.SemaphoreType.DMA((len(PIECES), 28)),
            pltpu.SemaphoreType.DMA((ROWS - 1,)),
            pltpu.SemaphoreType.DMA((ROWS - 1,)),
        ],
        compiler_params=pltpu.CompilerParams(
            collective_id=0, has_side_effects=True, vmem_limit_bytes=67043328
        ),
    )(error, observed_surpass_tally)
    return energy[None], skill[None]


def solution(mesh):
    return jax.shard_map(
        on_device,
        mesh=mesh,
        in_specs=(P("mem", "row", None), P("row", None)),
        out_specs=(P(None, None, "row", "mem"), P("mem", None, None)),
        check_vma=False,
    )
```

time: 308 us -> 189 us (0.61)
  waiting for transfers between devices: 190 us -> 0 us
  Pallas kernels: 0 us -> 181 us
  other arithmetic: 41.7 us -> 3.92 us
  starting transfers between devices: 37.2 us -> 0 us
  blocking collectives: 17.6 us -> 0 us
  between operations: 15.5 us -> 0.64 us
    pallas_call x0 -> x1, Pallas kernels: none -> 181 us  [on_device(): pl.pallas_call(kernel, out_shape=(jax.ShapeDtypeStruct((LEVELS + 1, H, 12...]
    reduce_scatter x1 -> x0, waiting for transfers between devices: 101 us -> none  [on_device(): summed = lax.psum_scatter(stacked, 'mem', scatter_dimension=3, tiled=True)]
    ppermute x14 -> x0, waiting for transfers between devices: 88.8 us -> none  [the longest x7 62.8 us: extended(): after = lax.ppermute(first, axis, down)]
    ppermute x14 -> x0, starting transfers between devices: 37.2 us -> none  [the longest x7 27.9 us: extended(): before = lax.ppermute(last, axis, up)]
    psum x1 -> x0, blocking collectives: 17.6 us -> none  [on_device(): sum_totals, sum_counts = lax.psum((local_totals, local_counts), 'row')]
    unnamed x7 -> x0, other arithmetic: 16.2 us -> none
    add x7 -> x0, other arithmetic: 14.5 us -> none  [column_pass(): result + KERNEL[index] * padded[:, index * spacing:index * spacing + brea...]
    reduce_sum x2 -> x0, other arithmetic: 6.7 us -> none  [the longest x1 3.82 us: on_device(): cumulative_accumulations.append(jnp.sum(squared))]
  transfers between devices with their start and end apart: 15 -> 0, of which waited for: 15 -> 0; matrix products, arithmetic and copies ran while one was open for 2% -> 0% of each run, Pallas kernels for 0% -> 0%
where the time goes in v1:
time: 189 us; the launch traced here: 188 us
  Pallas kernels  181 us (96%)
  other arithmetic  3.92 us (2%)
  local copies, waits for them, and re-layouts  3.05 us (2%)
    pallas_call x1, Pallas kernels, on_device(): pl.pallas_call(kernel, out_shape=(jax.ShapeDtypeStruct((LEVELS + 1, H, 12...  181 us
    sub x1, other arithmetic, on_device(): (predicted_surpass_tally[0] > 0).astype(F32)  3.92 us

profile of v1, /device:TPU:6, one launch (start us, length us, event | category | flops | bytes accessed | tf_op | source)
XLA Modules:
  0.0 188.4 jit_solution(8698277274769040488)
XLA Ops:
  0.6 3.9 %bitcast_subtract_fusion.e_ref = f32[128,4096]{1,0:T(8,128)} fusion(s32[128,4096]{1,0:T(8,128)} %obs_ref.1, s32[1,128,4096]{2,1,0:T(8,128)} %param.2), kind=kLoop, calls=%fused_computation | loop fusion | flops 2621440 | bytes 6291456 | tf_op jit(solution)/shard_map/sub | solution.py:405
  4.5 180.8 %shard_map.41 = (f32[8,128,128]{2,1,0:T(8,128)}, f32[1,8]{1,0:T(1,128)}) custom-call(f32[128,4096]{1,0:T(8,128)} %bitcast_subtract_fusion.e_ref, s32[128,4096]{1,0:T(8,128)} %obs_ref.1), custom_call_target="tpu_custom_call" | custom-call | tf_op jit(solution)/shard_map/pallas_call | solution.py:407
  185.4 1.9 copy.6
  187.2 1.2 copy.7

commit v2 on v1

--- a/solution.py
+++ b/solution.py
@@ -21,6 +21,7 @@
 TAPS = (1.0 / 16.0, 4.0 / 16.0, 6.0 / 16.0, 4.0 / 16.0, 1.0 / 16.0)
 WEIGHTS = [4.0 ** min(k + 1, LEVELS) for k in range(LEVELS + 1)]
 PAD = 128
+ROW_UNROLL, COL_UNROLL = 8, 7
 
 SLOT_ROW = (128, 384, 0, 512)
 HALO = (
@@ -30,20 +31,26 @@
     (1, -1, 16, 48),
     (0, 1, 0, 64),
     (1, -1, 64, 64),
-    (2, 2, 32, 96),
-    (3, -2, 0, 96),
-    (2, 2, 0, 32),
-    (3, -2, 96, 32),
+    (2, 1, 64, 64),
+    (3, -1, 0, 64),
+    (2, 1, 32, 32),
+    (3, -1, 64, 32),
+    (2, 1, 0, 32),
+    (3, -1, 96, 32),
 )
+OWN = 6
 PIECES = [[(k, 0), (k, 32), (k, 64), (k, 96)] for k in range(6)]
 PIECES += [[(6, 32), (6, 64), (7, 32), (7, 64)], [(6, 0), (6, 96), (7, 0), (7, 96)]]
 BLOCK = 32
+STRIP = 16
+STRIPS = (7, 0, 6, 1, 5, 2, 4, 3)
+DEPTH = 4
 
 
 def kernel(
-    e_ref, obs_ref, out_ref, skill_ref,
-    halo, ext, ub, sb, part, pair, ring1, ring2, xr, rm, rm7, xe, xi, ci, ce, obuf, acc, peers,
-    osem, zsend, zrecv, psend, precv, ksend, krecv,
+    pred_ref, obs_ref, out_ref, skill_ref,
+    e_ref, pbuf, obuf, halo, ext, ub, sb, part, pair, ring1, ring2, xr, rm, rm7, xe, xi, ci, ce, acc, peers,
+    psem, osem, zsend, zrecv, psend, precv, ksend, krecv,
 ):
     mem, row = lax.axis_index("mem"), lax.axis_index("row")
     c, y, x = lax.rem(mem, 2), lax.rem(mem // 2, SIDE), mem // (2 * SIDE)
@@ -62,11 +69,10 @@
     sibling = (at(x, y, 1 - c), row)
 
     barrier = pltpu.get_barrier_semaphore()
-    partners = [along_z(d) for d in range(1, ROWS)] + [sibling]
+    partners = [along_z(1), along_z(-1), sibling]
     partners += [along(axis, d) for axis in "xy" for d in (1, -1)]
     for partner in partners:
         pl.semaphore_signal(barrier, inc=1, device_id=partner, device_id_type=MESH)
-    pl.semaphore_wait(barrier, len(partners))
 
     sends = []
 
@@ -78,14 +84,57 @@
         sends.append(copy)
         return copy
 
-    halos = []
-    for n, (slot, step, first, rows) in enumerate(HALO):
+    halos = {}
+
+    def send_rows(n):
+        slot, step, first, rows = HALO[n]
         span = pl.ds(first, rows)
-        halos.append(remote(e_ref.at[span, :], halo.at[slot, span, :], zsend.at[n], zrecv.at[n], along_z(step)))
+        src = e_ref.at[span, :] if n < OWN else halo.at[slot - 2, span, :]
+        halos[n] = remote(src, halo.at[slot, span, :], zsend.at[n], zrecv.at[n], along_z(step))
+
+    def fetch(n):
+        span = pl.ds(STRIPS[n] * STRIP, STRIP)
+        slot = n % DEPTH
+        return (
+            pltpu.make_async_copy(pred_ref.at[span, :], pbuf.at[slot], psem.at[slot]),
+            pltpu.make_async_copy(obs_ref.at[span, :], obuf.at[slot], osem.at[slot]),
+        )
+
+    acc[...] = jnp.zeros_like(acc)
+    for n in range(DEPTH):
+        for copy in fetch(n):
+            copy.start()
+    for n, strip in enumerate(STRIPS):
+        for copy in fetch(n):
+            copy.wait()
+        first, slot = strip * STRIP, n % DEPTH
+
+        @pl.loop(0, W // 512)
+        def _(i):
+            lanes = pl.ds(pl.multiple_of(i * 512, 512), 512)
+            seen = jnp.where(obuf[slot, :, lanes] > 0, 1.0, 0.0)
+            error = jnp.where(pbuf[slot, :, lanes] > 0, 1.0, 0.0) - seen
+            e_ref[first : first + STRIP, lanes] = error
+            ext[256 + first : 256 + first + STRIP, lanes] = error.astype(BF16)
+            folded = seen[:, 0:128] + seen[:, 128:256] + seen[:, 256:384] + seen[:, 384:512]
+            acc[LEVELS + 1] += jnp.sum(folded.reshape(STRIP // 8, 8, 128), axis=0)
+
+        if n + DEPTH < len(STRIPS):
+            for copy in fetch(n + DEPTH):
+                copy.start()
+        if n == 1:
+            pl.semaphore_wait(barrier, len(partners))
+            send_rows(0)
+            send_rows(1)
+    for n in range(2, OWN):
+        send_rows(n)
+
+    def arrive(*numbers):
+        for n in numbers:
+            halos[n].wait_recv()
 
     def take(n):
         slot, _, first, rows = HALO[n]
-        halos[n].wait_recv()
 
         @pl.loop(0, W // 512)
         def _(i):
@@ -97,11 +146,8 @@
     @pl.loop(0, W // 512)
     def _(i):
         lanes = pl.ds(pl.multiple_of(i * 512, 512), 512)
-        ext[256:384, lanes] = e_ref[:, lanes].astype(BF16)
         for first, rows in ((0, 32), (128, 128), (384, 128), (608, 32)):
             ext[first : first + rows, lanes] = jnp.zeros((rows, 512), BF16)
-
-    acc[...] = jnp.zeros_like(acc)
 
     def taps(load, spacing):
         a, b, m, d, e = (load((q - 2) * spacing) for q in range(5))
@@ -172,7 +218,7 @@
         def pick(ref, offset):
             return [ref[offset + first : offset + first + rows, :] for first, rows in spans]
 
-        @pl.loop(0, TILES)
+        @pl.loop(0, TILES, unroll=ROW_UNROLL)
         def _(t):
             lanes = pl.ds(pl.multiple_of(t * TILE, TILE), TILE)
             left = jnp.concatenate(pick(ops, 0) + pick(ops, H), axis=0)
@@ -219,7 +265,7 @@
 
         near_left, whole, near_right = slice(256 - reach, 256), slice(0, 256), slice(0, reach)
 
-        @pl.loop(1, TILES - 1)
+        @pl.loop(1, TILES - 1, unroll=COL_UNROLL)
         def _(t):
             left = lhs([(t - 1, near_left), (t, whole), (t + 1, near_right)])
             depth = slice(256 - reach, 512 + reach)
@@ -342,49 +388,59 @@
     for level in range(1, LEVELS):
         column_operators(level)
         if level == 1:
+            arrive(0, 1)
             take(0), take(1)
-        if level == 4:
+        if level == 3:
+            arrive(2, 3)
+            send_rows(6), send_rows(7)
             take(2), take(3)
-        if level == 6:
+        if level == 5:
+            arrive(4, 5)
+            for n in range(8, 12):
+                send_rows(n)
             take(4), take(5)
         level_pass(level, everything)
         tick(level - 2)
         begin(level - 1)
 
-    @pl.loop(0, W // 512)
-    def _(i):
-        copy = pltpu.make_async_copy(obs_ref.at[:, pl.ds(pl.multiple_of(i * 512, 512), 512)], obuf, osem)
-        copy.start()
-        copy.wait()
-        seen = jnp.where(obuf[...] > 0, 1.0, 0.0)
-        acc[LEVELS + 1] += jnp.sum(jnp.sum(seen.reshape(16, 8, 4, 128), axis=0), axis=1)
-
     column_operators(LEVELS)
     while any(position[p] < 5 for p in range(6)):
         tick(5)
 
-    take(6), take(7)
+    arrive(6, 7, 8, 9)
+    take(6), take(7), take(8), take(9)
     level_pass(LEVELS, [(32, 64)])
     begin(6)
     tick(6)
     tick(6)
-    take(8), take(9)
+    arrive(10, 11)
+    take(10), take(11)
     level_pass(LEVELS, [(0, 32), (96, 32)])
     begin(7)
 
-    tallies = [
-        remote(acc, peers.at[d - 1], ksend.at[d - 1], krecv.at[d - 1], along_z(d)) for d in range(1, ROWS)
-    ]
-    while any(position[p] < 5 for p in position):
+    def relay(hop):
+        for step in (1, -1):
+            if step == -1 and hop == ROWS // 2:
+                continue
+            if hop > 1:
+                flights["tally", hop - 1, step].wait_recv()
+            src = acc if hop == 1 else peers.at[(step * (hop - 1)) % ROWS]
+            slot = (step * hop) % ROWS
+            flights["tally", hop, step] = remote(src, peers.at[slot], ksend.at[slot], krecv.at[slot], along_z(step))
+
+    hop = 0
+    while any(position[p] < 5 for p in position) or hop < ROWS // 2:
+        if hop < ROWS // 2:
+            hop += 1
+            relay(hop)
         tick(7)
-
-    for copy in tallies:
-        copy.wait_recv()
+    flights["tally", ROWS // 2, 1].wait_recv()
+    flights["tally", ROWS // 2 - 1, -1].wait_recv()
     cells = float(ROWS * H * W)
 
     def total(k):
         value = acc[k]
-        for d in range(ROWS - 1):
+        for d in range(1, ROWS):
             value = value + peers[d, k]
         return jnp.sum(jnp.sum(value, axis=0, keepdims=True), axis=1, keepdims=True)
 
@@ -402,7 +458,6 @@
 
 
 def on_device(predicted_surpass_tally, observed_surpass_tally):
-    error = (predicted_surpass_tally[0] > 0).astype(F32) - (observed_surpass_tally > 0).astype(F32)
     vmem = pl.BlockSpec(memory_space=pltpu.VMEM)
     energy, skill = pl.pallas_call(
         kernel,
@@ -410,9 +465,12 @@
             jax.ShapeDtypeStruct((LEVELS + 1, H, 128), F32),
             jax.ShapeDtypeStruct((1, LEVELS + 1), F32),
         ),
-        in_specs=[vmem, pl.BlockSpec(memory_space=pl.ANY)],
+        in_specs=[pl.BlockSpec(memory_space=pl.ANY)] * 2,
         out_specs=(vmem, vmem),
         scratch_shapes=[
+            pltpu.VMEM((H, W), F32),
+            pltpu.VMEM((DEPTH, STRIP, W), jnp.int32),
+            pltpu.VMEM((DEPTH, STRIP, W), jnp.int32),
             pltpu.VMEM((4, H, W), F32),
             pltpu.VMEM((5 * H, W), BF16),
             pltpu.VMEM((TILES, 2 * H, TILE), BF16),
@@ -428,21 +486,21 @@
             pltpu.VMEM((2, 768 + 2 * PAD, TILE), F32),
             pltpu.VMEM((2, 768, TILE), BF16),
             pltpu.VMEM((2, 512, 512), BF16),
-            pltpu.VMEM((H, 512), jnp.int32),
             pltpu.VMEM((LEVELS + 2, 8, 128), F32),
-            pltpu.VMEM((ROWS - 1, LEVELS + 2, 8, 128), F32),
-            pltpu.SemaphoreType.DMA,
+            pltpu.VMEM((ROWS, LEVELS + 2, 8, 128), F32),
+            pltpu.SemaphoreType.DMA((DEPTH,)),
+            pltpu.SemaphoreType.DMA((DEPTH,)),
             pltpu.SemaphoreType.DMA((len(HALO),)),
             pltpu.SemaphoreType.DMA((len(HALO),)),
             pltpu.SemaphoreType.DMA((len(PIECES), 28)),
             pltpu.SemaphoreType.DMA((len(PIECES), 28)),
-            pltpu.SemaphoreType.DMA((ROWS - 1,)),
-            pltpu.SemaphoreType.DMA((ROWS - 1,)),
+            pltpu.SemaphoreType.DMA((ROWS,)),
+            pltpu.SemaphoreType.DMA((ROWS,)),
         ],
         compiler_params=pltpu.CompilerParams(
             collective_id=0, has_side_effects=True, vmem_limit_bytes=67043328
         ),
-    )(error, observed_surpass_tally)
+    )(predicted_surpass_tally[0], observed_surpass_tally)
     return energy[None], skill[None]
 
 

time: 189 us -> 130 us (0.69)
  Pallas kernels: 181 us -> 126 us
  other arithmetic: 3.92 us -> 0 us
    pallas_call x1, Pallas kernels: 181 us -> 126 us  [on_device(): pl.pallas_call(kernel, out_shape=(jax.ShapeDtypeStruct((LEVELS + 1, H, 12...]
    sub x1 -> x0, other arithmetic: 3.92 us -> none  [on_device(): (predicted_surpass_tally[0] > 0).astype(F32)]
where the time goes in v2:
time: 130 us
  Pallas kernels  126 us (97%)
  local copies, waits for them, and re-layouts  2.98 us (2%)
    pallas_call x1, Pallas kernels, on_device(): pl.pallas_call(kernel, out_shape=(jax.ShapeDtypeStruct((LEVELS + 1, H, 12...  126 us
    unnamed x2, local copies, waits for them, and re-layouts  2.98 us

profile of v2, /device:TPU:6, one launch (start us, length us, event | category | flops | bytes accessed | tf_op | source)
XLA Modules:
  0.0 129.8 jit_solution(1991232901095001011)
XLA Ops:
  0.6 126.2 %shard_map.41 = (f32[8,128,128]{2,1,0:T(8,128)}, f32[1,8]{1,0:T(1,128)}) custom-call(s32[128,4096]{1,0:T(8,128)} %bitcast.3, s32[128,4096]{1,0:T(8,128)} %obs_ref.1), custom_call_target="tpu_custom_call" | custom-call | tf_op jit(solution)/shard_map/pallas_call | solution.py:462
  126.8 1.9 %copy.6 = f32[1,8,128,128]{3,2,1,0:T(8,128)} copy(f32[1,8,128,128]{3,2,1,0:T(8,128)} %bitcast.4) | data formatting | bytes 1048576
  128.7 1.1 copy.7

commit v3 on v2

--- a/solution.py
+++ b/solution.py
@@ -21,7 +21,8 @@
 TAPS = (1.0 / 16.0, 4.0 / 16.0, 6.0 / 16.0, 4.0 / 16.0, 1.0 / 16.0)
 WEIGHTS = [4.0 ** min(k + 1, LEVELS) for k in range(LEVELS + 1)]
 PAD = 128
-ROW_UNROLL, COL_UNROLL = 8, 7
+ROW_UNROLL = 8
+STACK = (1, 1, 1, 1, 1, 1, 1, 7, 7)
 
 SLOT_ROW = (128, 384, 0, 512)
 HALO = (
@@ -35,16 +36,22 @@
     (3, -1, 0, 64),
     (2, 1, 32, 32),
     (3, -1, 64, 32),
-    (2, 1, 0, 32),
-    (3, -1, 96, 32),
+    (2, 1, 16, 16),
+    (3, -1, 96, 16),
+    (2, 1, 0, 16),
+    (3, -1, 112, 16),
 )
 OWN = 6
-PIECES = [[(k, 0), (k, 32), (k, 64), (k, 96)] for k in range(6)]
-PIECES += [[(6, 32), (6, 64), (7, 32), (7, 64)], [(6, 0), (6, 96), (7, 0), (7, 96)]]
+PIECES = [(32, [(k, 0), (k, 32), (k, 64), (k, 96)]) for k in range(6)]
+PIECES += [
+    (32, [(6, 32), (6, 64), (7, 32), (7, 64)]),
+    (16, [(6, 16), (6, 96), (7, 16), (7, 96)]),
+    (16, [(6, 0), (6, 112), (7, 0), (7, 112)]),
+]
 BLOCK = 32
 STRIP = 16
 STRIPS = (7, 0, 6, 1, 5, 2, 4, 3)
-DEPTH = 4
+DEPTH = 2
 
 
 def kernel(
@@ -209,11 +216,27 @@
             xe[dst, PAD : PAD + 512, lanes] = new
             ce[0, :, lanes], ce[1, :, lanes] = split(new)
 
-    def level_pass(level, spans):
+    def pair_copy(p, i, group):
+        height, blocks = PIECES[p]
+        k, first = blocks[i]
+        half = pl.ds(group * (SIDE // 2), SIDE // 2)
+        rows = pl.ds(first, height)
+        return pltpu.make_async_remote_copy(
+            src_ref=part.at[k, 1 - c, half, :, rows, :],
+            dst_ref=pair.at[k, half, :, rows, :],
+            send_sem=psend.at[p, 2 * i + group],
+            recv_sem=precv.at[p, 2 * i + group],
+            device_id=sibling,
+            device_id_type=MESH,
+        )
+
+    def level_pass(level, spans, piece):
         reach = 256 if level == LEVELS else 128
         height = sum(rows for _, rows in spans)
         ops = rm7 if level == LEVELS else rm.at[level - 1]
         depth = slice(0, 640) if level == LEVELS else slice(128, 512)
+        late = piece > 6
+        stack = STACK[piece]
 
         def pick(ref, offset):
             return [ref[offset + first : offset + first + rows, :] for first, rows in spans]
@@ -221,9 +244,32 @@
         @pl.loop(0, TILES, unroll=ROW_UNROLL)
         def _(t):
             lanes = pl.ds(pl.multiple_of(t * TILE, TILE), TILE)
-            left = jnp.concatenate(pick(ops, 0) + pick(ops, H), axis=0)
-            both = jnp.dot(left, ext[depth, lanes], preferred_element_type=F32)
-            high, low = split(both[:height] + both[height:])
+            if late:
+                left = jnp.concatenate(pick(ops, 0) + pick(ops, H), axis=0)
+                left = jnp.concatenate([left[:, 0:32], left[:, 608:640]], axis=1)
+                right = jnp.concatenate([ext[0:32, lanes], ext[608:640, lanes]], axis=0)
+            else:
+                left, right = ops[...], ext[depth, lanes]
+            both = jnp.dot(left, right, preferred_element_type=F32)
+            value = both[: left.shape[0] // 2] + both[left.shape[0] // 2 :]
+            if late:
+                value = value + jnp.concatenate(
+                    [
+                        jnp.concatenate(
+                            [part[LEVELS, core, t // SIDE, t % SIDE, first : first + rows, :] for core in range(2)], axis=1
+                        )
+                        for first, rows in spans
+                    ],
+                    axis=0,
+                )
+            elif piece == 6:
+                for first in (0, 96):
+                    for core in range(2):
+                        part[LEVELS, core, t // SIDE, t % SIDE, first : first + 32, :] = value[
+                            first : first + 32, core * 128 : core * 128 + 128
+                        ]
+                value = value[32:96]
+            high, low = split(value)
             done = 0
             for first, rows in spans:
                 ub[t, first : first + rows, :] = high[done : done + rows]
@@ -265,14 +311,6 @@
 
         near_left, whole, near_right = slice(256 - reach, 256), slice(0, 256), slice(0, reach)
 
-        @pl.loop(1, TILES - 1, unroll=COL_UNROLL)
-        def _(t):
-            left = lhs([(t - 1, near_left), (t, whole), (t + 1, near_right)])
-            depth = slice(256 - reach, 512 + reach)
-            both = jnp.dot(left, ci[0, depth, :], preferred_element_type=F32)
-            cross = jnp.dot(left[:height], ci[1, depth, :], preferred_element_type=F32)
-            finish(t, both, cross)
-
         for t, tiles, out, depth in (
             (0, [(0, whole), (1, near_right)], slice(0, 256), slice(0, 256 + reach)),
             (TILES - 1, [(TILES - 2, near_left), (TILES - 1, whole)], slice(256, 512), slice(256 - reach, 512)),
@@ -283,11 +321,27 @@
             cross = lax.dot_general(left[:height], ce[1, out, depth], dims, preferred_element_type=F32)
             finish(t, both, cross)
 
+        @pl.loop(0, 2)
+        def _(group):
+            depth = slice(256 - reach, 512 + reach)
+            for j in range(0, TILES // 2 - 1, stack):
+                tiles = [group * (TILES // 2 - 1) + (j + n + 1) for n in range(stack)]
+                parts = [lhs([(t - 1, near_left), (t, whole), (t + 1, near_right)]) for t in tiles]
+                left = jnp.concatenate(parts, axis=0)
+                both = jnp.dot(left, ci[0, depth, :], preferred_element_type=F32)
+                left = jnp.concatenate([one[:height] for one in parts], axis=0)
+                cross = jnp.dot(left, ci[1, depth, :], preferred_element_type=F32)
+                for n, t in enumerate(tiles):
+                    finish(t, both[2 * n * height : 2 * (n + 1) * height], cross[n * height : (n + 1) * height])
+            for i in range(4):
+                pair_copy(piece, i, group).start()
+
     flights = {}
 
     def block_of(p, i, axis, pos, stage):
-        k, first = PIECES[p][i]
-        rows = pl.ds(first, BLOCK)
+        height, blocks = PIECES[p]
+        k, first = blocks[i]
+        rows = pl.ds(first, height)
         if stage == 1:
             if axis == "y":
                 return part.at[k, c, :, pos, rows, :]
@@ -302,34 +356,38 @@
     def spot(axis, step):
         return lax.rem((y if axis == "y" else x) + step + SIDE, SIDE)
 
-    def pair_start(p):
-        for i, (k, first) in enumerate(PIECES[p]):
-            rows = pl.ds(first, BLOCK)
-            flights[p, 0, i] = remote(
-                part.at[k, 1 - c, :, :, rows, :], pair.at[k, :, :, rows, :], psend.at[p, i], precv.at[p, i], sibling
-            )
-
     def ring_copy(p, stage, half, n, i, pos, step):
         axis = axis_of(half, stage)
-        landing = (ring1 if stage == 1 else ring2).at[p, half, n]
-        sem = 4 + (stage - 1) * 12 + half * 6 + n
+        height = PIECES[p][0]
+        slot, base = (p, 0) if p < 8 else (p - 1, height)
+        if stage == 1:
+            landing = ring1.at[slot, half, n, :, pl.ds(base, height), :]
+        else:
+            landing = ring2.at[slot, half, n, pl.ds(base, height), :]
+        sem = 8 + (stage - 1) * 12 + half * 6 + n
         flights[p, stage, half, n] = remote(
             block_of(p, i, axis, spot(axis, pos), stage), landing, psend.at[p, sem], precv.at[p, sem], along(axis, step)
         )
 
-    def ring_start(p, stage):
-        for half in range(2):
-            i0, i1 = 2 * half, 2 * half + 1
-            ring_copy(p, stage, half, 0, i0, 2, 1)
-            ring_copy(p, stage, half, 1, i1, 2, -1)
-            ring_copy(p, stage, half, 2, i1, 1, 1)
-            ring_copy(p, stage, half, 3, i0, -1, -1)
+    def ring_start(p, stage, i):
+        half = i // 2
+        if i % 2 == 0:
+            ring_copy(p, stage, half, 0, i, 2, 1)
+            ring_copy(p, stage, half, 3, i, -1, -1)
+        else:
+            ring_copy(p, stage, half, 1, i, 2, -1)
+            ring_copy(p, stage, half, 2, i, 1, 1)
 
     def ring_add(p, stage, half, n, i, pos):
         axis = axis_of(half, stage)
         flights[p, stage, half, n].wait_recv()
         block = block_of(p, i, axis, spot(axis, pos), stage)
-        block[...] = block[...] + (ring1 if stage == 1 else ring2)[p, half, n]
+        height = PIECES[p][0]
+        slot, base = (p, 0) if p < 8 else (p - 1, height)
+        if stage == 1:
+            block[...] = block[...] + ring1[slot, half, n, :, base : base + height, :]
+        else:
+            block[...] = block[...] + ring2[slot, half, n, base : base + height, :]
 
     def ring_middle(p, stage):
         for half in range(2):
@@ -339,38 +397,38 @@
             ring_add(p, stage, half, 1, i1, -1)
             ring_copy(p, stage, half, 5, i1, -1, -1)
 
-    def ring_end(p, stage):
-        for half in range(2):
-            i0, i1 = 2 * half, 2 * half + 1
-            ring_add(p, stage, half, 3, i0, 0)
-            ring_add(p, stage, half, 2, i1, 0)
-            ring_add(p, stage, half, 4, i0, 0)
-            ring_add(p, stage, half, 5, i1, 0)
+    def ring_end(p, stage, i):
+        half = i // 2
+        ring_add(p, stage, half, 3 if i % 2 == 0 else 2, i, 0)
+        ring_add(p, stage, half, 4 if i % 2 == 0 else 5, i, 0)
 
     def advance(p, step):
-        if step == 0:
-            pair_start(p)
-        elif step == 1:
-            for i, (k, first) in enumerate(PIECES[p]):
-                flights[p, 0, i].wait_recv()
-
-                @pl.loop(0, SIDE)
-                def _(j):
-                    rows = pl.ds(first, BLOCK)
-                    part[k, c, j, :, rows, :] = part[k, c, j, :, rows, :] + pair[k, j, :, rows, :]
-
-            ring_start(p, 1)
+        height, blocks = PIECES[p]
+        if step == 1:
+            for i, (k, first) in enumerate(blocks):
+                rows = pl.ds(first, height)
+                for group in range(2):
+                    copy = pair_copy(p, i, group)
+                    copy.wait_recv()
+                    sends.append(copy)
+
+                    @pl.loop(2 * group, 2 * group + 2)
+                    def _(j):
+                        part[k, c, j, :, rows, :] = part[k, c, j, :, rows, :] + pair[k, j, :, rows, :]
+
+                ring_start(p, 1, i)
         elif step == 2:
             ring_middle(p, 1)
         elif step == 3:
-            ring_end(p, 1)
-            ring_start(p, 2)
+            for i in range(4):
+                ring_end(p, 1, i)
+                ring_start(p, 2, i)
         elif step == 4:
             ring_middle(p, 2)
         elif step == 5:
-            ring_end(p, 2)
-            for k, first in PIECES[p]:
-                out_ref[k, first : first + BLOCK, :] = part[k, c, x, y, pl.ds(first, BLOCK), :]
+            for i, (k, first) in enumerate(blocks):
+                ring_end(p, 2, i)
+                out_ref[k, first : first + height, :] = part[k, c, x, y, pl.ds(first, height), :]
 
     position = {}
 
@@ -379,10 +437,6 @@
             if p <= limit and position[p] < 5:
                 position[p] += 1
                 advance(p, position[p])
-
-    def begin(p):
-        position[p] = 0
-        advance(p, 0)
 
     everything = [(0, H)]
     for level in range(1, LEVELS):
@@ -396,12 +450,12 @@
             take(2), take(3)
         if level == 5:
             arrive(4, 5)
-            for n in range(8, 12):
+            for n in range(8, len(HALO)):
                 send_rows(n)
             take(4), take(5)
-        level_pass(level, everything)
+        level_pass(level, everything, level - 1)
         tick(level - 2)
-        begin(level - 1)
+        position[level - 1] = 0
 
     column_operators(LEVELS)
     while any(position[p] < 5 for p in range(6)):
@@ -409,14 +463,18 @@
 
     arrive(6, 7, 8, 9)
     take(6), take(7), take(8), take(9)
-    level_pass(LEVELS, [(32, 64)])
-    begin(6)
-    tick(6)
+    level_pass(LEVELS, [(32, 64)], 6)
+    position[6] = 0
     tick(6)
     arrive(10, 11)
     take(10), take(11)
-    level_pass(LEVELS, [(0, 32), (96, 32)])
-    begin(7)
+    level_pass(LEVELS, [(16, 16), (96, 16)], 7)
+    position[7] = 0
+    tick(7)
+    arrive(12, 13)
+    take(12), take(13)
+    level_pass(LEVELS, [(0, 16), (112, 16)], 8)
+    position[8] = 0
 
     def relay(hop):
         for step in (1, -1):
@@ -433,7 +491,7 @@
         if hop < ROWS // 2:
             hop += 1
             relay(hop)
-        tick(7)
+        tick(8)
     flights["tally", ROWS // 2, 1].wait_recv()
     flights["tally", ROWS // 2 - 1, -1].wait_recv()
     cells = float(ROWS * H * W)
@@ -477,8 +535,8 @@
             pltpu.VMEM((TILES, H, TILE), F32),
             pltpu.VMEM((LEVELS + 1, 2, SIDE, SIDE, H, 128), F32),
             pltpu.VMEM((LEVELS + 1, SIDE, SIDE, H, 128), F32),
-            pltpu.VMEM((len(PIECES), 2, 6, SIDE, BLOCK, 128), F32),
-            pltpu.VMEM((len(PIECES), 2, 6, BLOCK, 128), F32),
+            pltpu.VMEM((len(PIECES) - 1, 2, 6, SIDE, BLOCK, 128), F32),
+            pltpu.VMEM((len(PIECES) - 1, 2, 6, BLOCK, 128), F32),
             pltpu.VMEM((2, 640 + 2 * PAD, 128), F32),
             pltpu.VMEM((LEVELS - 1, 2 * H, 384), BF16),
             pltpu.VMEM((2 * H, 640), BF16),
@@ -492,8 +550,8 @@
             pltpu.SemaphoreType.DMA((DEPTH,)),
             pltpu.SemaphoreType.DMA((len(HALO),)),
             pltpu.SemaphoreType.DMA((len(HALO),)),
-            pltpu.SemaphoreType.DMA((len(PIECES), 28)),
-            pltpu.SemaphoreType.DMA((len(PIECES), 28)),
+            pltpu.SemaphoreType.DMA((len(PIECES), 32)),
+            pltpu.SemaphoreType.DMA((len(PIECES), 32)),
             pltpu.SemaphoreType.DMA((ROWS,)),
             pltpu.SemaphoreType.DMA((ROWS,)),
         ],

time: 130 us -> 130 us (level)
  no operation moved by 1% of the time
where the time goes in v3:
time: 130 us
  Pallas kernels  126 us (97%)
  local copies, waits for them, and re-layouts  2.98 us (2%)
    pallas_call x1, Pallas kernels, on_device(): pl.pallas_call(kernel, out_shape=(jax.ShapeDtypeStruct((LEVELS + 1, H, 12...  126 us
    unnamed x2, local copies, waits for them, and re-layouts  2.98 us

profile of v3, /device:TPU:6, one launch (start us, length us, event | category | flops | bytes accessed | tf_op | source)
XLA Modules:
  0.0 129.5 jit_solution(8586650152680916277)
XLA Ops:
  0.6 125.9 %shard_map.41 = (f32[8,128,128]{2,1,0:T(8,128)}, f32[1,8]{1,0:T(1,128)}) custom-call(s32[128,4096]{1,0:T(8,128)} %bitcast.3, s32[128,4096]{1,0:T(8,128)} %obs_ref.1), custom_call_target="tpu_custom_call" | custom-call | tf_op jit(solution)/shard_map/pallas_call | solution.py:520
  126.5 1.9 %copy.6 = f32[1,8,128,128]{3,2,1,0:T(8,128)} copy(f32[1,8,128,128]{3,2,1,0:T(8,128)} %bitcast.4) | data formatting | bytes 1048576
  128.4 1.1 copy.7
